TPU v7x, 256 devices: a whole 4x4x8 slice. The times are simulated.
256 devices in a mesh: guide: 2 (over core), seq: 128 (over x, z, y).
Axes of the slice: x: 4, y: 4, z: 8, core: 2. Of those that a mesh axis runs over, the one named last changes fastest.
Arguments:
- hidden: bfloat16 [2, 24576, 3072], P('guide', 'seq'), may hold values from -6 to 6
- query_rows: bfloat16 [2, 24576, 1536], P('guide', 'seq'), may hold values from -6 to 6
- key_rows: bfloat16 [2, 24576, 1536], P('guide', 'seq'), may hold values from -6 to 6
- value_rows: bfloat16 [2, 24576, 1536], P('guide', 'seq'), may hold values from -6 to 6
- text_lengths: int32 [2, 32], P('guide'), may hold values from 1 to 512, as said below
- q_gain: float32 [128], replicated, may hold values from 0.6 to 6
- k_gain: float32 [128], replicated, may hold values from 0.6 to 6
- o_weight: bfloat16 [1536, 3072], P('guide'), may hold values from -0.15625 to 0.15625
- layer_gate: float32 [2, 32, 3072], P('guide'), may hold values from -5 to 5
- final_shift: float32 [2, 32, 3072], P('guide'), may hold values from -3 to 3
- final_scale: float32 [2, 32, 3072], P('guide'), may hold values from -2.5 to 2.5
- final_weight: bfloat16 [3072, 64], replicated, may hold values from -0.109375 to 0.109375
- final_bias: float32 [64], replicated, may hold values from -3 to 3
- latents: float32 [8192, 64], P('seq', 'guide'), may hold values from -6 to 6
- step_delta: float32 [32], replicated, may hold values from -0.6 to -0.2
Outputs:
- new_latents: float32 [8192, 64], P('seq', 'guide')
- hidden_out: bfloat16 [2, 24576, 3072], P('guide', 'seq')
- hidden_rms: float32 [2, 32], P('guide')
- hidden_peak: float32 [2, 32], P('guide')
Inputs may be any that keep to these rules, and one draw needn't show every extreme that they name: `text_lengths`: some request of some half has all 512 text slots live.
All inputs are finite; a program needn't handle non-finite values.
Results may differ from a plain program's by a relative error of at most 0.015.
The roundings to bfloat16 on the way count: a program that leaves them out, or rounds other values in their place, can miss the bound.
Values may be sent and summed in bfloat16 or wider, within the bound.
A program may use at most 128 MiB of HBM per device.

v0:
```python
import math

import jax
import jax.numpy as jnp
from jax import lax
from jax.sharding import PartitionSpec as P

HD = 128
GROUP = 4
TXT_DEV = 128


guidance_weight = 3.5


def shifted(value, axis, steps):
    count = lax.axis_size(axis)
    initial, last = (max(0, -steps), min(count, count - steps))
    return lax.ppermute(value, axis, [(source, source + steps) for source in range(initial, last)])


def partner(block, axis, bit):
    count = lax.axis_size(axis)
    route = []
    for low in range(count):
        high = low | 1 << bit
        if high != low and high < count:
            route += [(low, high), (high, low)]
    return lax.ppermute(block, axis, route)


def normalize_heads(raw_rows, channel_gain, factor):
    values = raw_rows.astype(jnp.float32)
    inv_rms = lax.rsqrt(jnp.mean(values * values, axis=-1, keepdims=True) + 1e-06)
    return (values * inv_rms * channel_gain * factor).astype(jnp.bfloat16)


def key_mask(source, length, row_count):
    within = jnp.arange(row_count, dtype=jnp.int32)
    usable = (within >= TXT_DEV) | (source * TXT_DEV + within < length)
    return usable & (source >= 0) & (source < GROUP)


def attend(softmax_state, queries, arrived, usable):
    running_max, denominator, numerator = softmax_state
    scores = jnp.einsum("qhd,khd->hqk", queries, arrived[0], preferred_element_type=jnp.float32)
    scores = jnp.where(usable[None, None, :], scores, jnp.float32(-1e30))
    new_max = jnp.maximum(running_max, jnp.max(scores, axis=-1))
    rescale = jnp.exp(running_max - new_max)
    weights = jnp.exp(scores - new_max[..., None])
    denominator = denominator * rescale + jnp.sum(weights, axis=-1)
    numerator = numerator * rescale[..., None] + jnp.einsum(
        "hqk,khd->hqd", weights.astype(jnp.bfloat16), arrived[1], preferred_element_type=jnp.float32
    )
    return (new_max, denominator, numerator)


def guarded_attend(softmax_state, queries, arrived, source, length, row_count):
    inside = (source >= 0) & (source < GROUP)
    usable = key_mask(source, length, row_count)

    def with_block(state):
        return attend(state, queries, arrived, usable)

    def without_block(state):
        return state

    return lax.cond(inside, with_block, without_block, softmax_state)


def on_device(
    hidden,
    query_rows,
    key_rows,
    value_rows,
    text_lengths,
    q_gain,
    k_gain,
    o_weight,
    layer_gate,
    final_shift,
    final_scale,
    final_weight,
    final_bias,
    latents,
    step_delta,
):
    seq_rank = lax.axis_index("seq")
    guide_rank = lax.axis_index("guide")
    req_count = lax.axis_size("seq") // GROUP
    request = seq_rank % req_count
    position = seq_rank // req_count
    row_count = hidden.shape[1]
    width = hidden.shape[2]
    head_count = query_rows.shape[2] // HD
    length = text_lengths[0][request]
    queries = normalize_heads(
        query_rows[0].reshape(row_count, head_count, HD), q_gain, 1.0 / math.sqrt(HD)
    )
    keys_normed = normalize_heads(key_rows[0].reshape(row_count, head_count, HD), k_gain, 1.0)
    key_pair = jnp.stack([keys_normed, value_rows[0].reshape(row_count, head_count, HD)])
    softmax_state = (
        jnp.full((head_count, row_count), -1e30, jnp.float32),
        jnp.zeros((head_count, row_count), jnp.float32),
        jnp.zeros((head_count, row_count, HD), jnp.float32),
    )
    softmax_state = attend(softmax_state, queries, key_pair, key_mask(position, length, row_count))
    moving = key_pair
    for offset in range(1, GROUP):
        moving = shifted(moving, "seq", req_count)
        softmax_state = guarded_attend(
            softmax_state, queries, moving, position - offset, length, row_count
        )
    moving = key_pair
    for offset in range(1, GROUP):
        moving = shifted(moving, "seq", -req_count)
        softmax_state = guarded_attend(
            softmax_state, queries, moving, position + offset, length, row_count
        )
    denominator = softmax_state[1]
    numerator = softmax_state[2]
    attended = (
        (numerator / denominator[..., None])
        .transpose(1, 0, 2)
        .reshape(row_count, head_count * HD)
        .astype(jnp.bfloat16)
    )
    full_weight = lax.all_gather(o_weight, "guide", axis=0, tiled=True)
    projected = jnp.dot(attended, full_weight, preferred_element_type=jnp.float32)
    gate_row = layer_gate[0][request]
    hidden_new = (hidden[0].astype(jnp.float32) + gate_row[None, :] * projected).astype(
        jnp.bfloat16
    )
    widened = hidden_new.astype(jnp.float32)
    one_hot = (jnp.arange(req_count, dtype=jnp.int32) == request).astype(jnp.float32)
    square_vector = one_hot * jnp.sum(widened * widened)
    peak_vector = one_hot * jnp.max(jnp.abs(widened))
    square_sums = lax.psum(square_vector, "seq")
    peak_values = lax.pmax(peak_vector, "seq")
    hidden_rms = jnp.sqrt(square_sums / (GROUP * row_count * width) + 1e-06)
    image_rows = widened[TXT_DEV:]
    row_mean = jnp.mean(image_rows, axis=-1, keepdims=True)
    centered = image_rows - row_mean
    row_var = jnp.mean(centered * centered, axis=-1, keepdims=True)
    normed = centered * lax.rsqrt(row_var + 1e-06)
    modulated = (
        normed * (1.0 + final_scale[0][request][None, :]) + final_shift[0][request][None, :]
    ).astype(jnp.bfloat16)
    velocity = (
        jnp.dot(modulated, final_weight, preferred_element_type=jnp.float32) + final_bias[None, :]
    )
    half_ch = latents.shape[1]
    own_part = lax.dynamic_slice_in_dim(velocity, guide_rank * half_ch, half_ch, 1)
    sent_part = lax.dynamic_slice_in_dim(velocity, (1 - guide_rank) * half_ch, half_ch, 1)
    partner_vel = partner(sent_part, "guide", 0)
    conditional = jnp.where(guide_rank == 0, own_part, partner_vel)
    unconditional = jnp.where(guide_rank == 0, partner_vel, own_part)
    guided = unconditional + guidance_weight * (conditional - unconditional)
    new_latents = latents + step_delta[request] * guided
    return (new_latents, hidden_new[None], hidden_rms[None], peak_values[None])


def solution(mesh):
    return jax.shard_map(
        on_device,
        mesh=mesh,
        in_specs=(
            P("guide", "seq", None),
            P("guide", "seq", None),
            P("guide", "seq", None),
            P("guide", "seq", None),
            P("guide", None),
            P(),
            P(),
            P("guide", None),
            P("guide", None, None),
            P("guide", None, None),
            P("guide", None, None),
            P(),
            P(),
            P("seq", "guide"),
            P(),
        ),
        out_specs=(P("seq", "guide"), P("guide", "seq", None), P("guide", None), P("guide", None)),
        check_vma=False,
    )
```

profile of v0, /device:TPU:8, one launch (start us, length us, event | category | flops | bytes accessed | tf_op | source)
XLA Modules:
  0.0 823.2 jit_solution(6516606013157790800)
XLA Ops:
  8.7 1.5 reshape.123
  10.1 2.2 stack_reshape_squeeze.3
  13.5 1.4 multiply_convert_fusion
  15.2 1.3 copy.61
  16.5 4.4 collective-permute-start
  21.0 1.3 collective-permute-start.3
  22.3 1.5 reshape.121
  24.2 2.3 multiply_convert_fusion.1
  26.5 18.9 %collective-permute-done = bf16[2,192,12,128]{3,1,2,0:T(8,128)(2,1)} collective-permute-done((bf16[2,192,12,128]{3,1,2,0:T(8,128)(2,1)}, bf16[2,192,12,128]{3,1,2,0:T(8,128)(2,1)}, u32[]{:S(2)}, u32[]{:S(2)}) %collective-permute-start) | collective-permute-done | bytes 1179680 | tf_op jit(solution)/shard_map/ppermute | solution.py:19
  45.4 5.4 collective-permute-start.1
  50.9 1.3 collective-permute-start.4
  52.7 1.5 squeeze_stack_reshape_squeeze.3
  56.7 17.8 %collective-permute-done.1 = bf16[2,192,12,128]{3,1,2,0:T(8,128)(2,1)} collective-permute-done((bf16[2,192,12,128]{3,1,2,0:T(8,128)(2,1)}, bf16[2,192,12,128]{3,1,2,0:T(8,128)(2,1)}, u32[]{:S(2)}, u32[]{:S(2)}) %collective-permute-start.1) | collective-permute-done | bytes 1179680 | tf_op jit(solution)/shard_map/ppermute | solution.py:19
  74.5 5.4 collective-permute-start.2
  79.9 1.3 collective-permute-start.5
  85.0 1.5 constant_dynamic-slice_fusion.3
  86.5 1.6 dynamic-slice_add_fusion
  88.0 14.7 %collective-permute-done.2 = bf16[2,192,12,128]{3,1,2,0:T(8,128)(2,1)} collective-permute-done((bf16[2,192,12,128]{3,1,2,0:T(8,128)(2,1)}, bf16[2,192,12,128]{3,1,2,0:T(8,128)(2,1)}, u32[]{:S(2)}, u32[]{:S(2)}) %collective-permute-start.2) | collective-permute-done | bytes 1179680 | tf_op jit(solution)/shard_map/ppermute | solution.py:19
  102.7 4.5 conditional.9
  102.7 1.6 select_reduce_fusion.3
  104.9 2.3 convolution_add_fusion.3
  107.8 4.5 conditional.10
  107.8 1.6 select_reduce_fusion.4
  110.0 2.3 convolution_add_fusion.4
  112.3 4.7 conditional.11
  112.4 1.6 select_reduce_fusion.5
  114.5 2.3 convolution_add_fusion.5
  117.1 6.1 fusion.100
  124.2 1.2 abs_reduce_fusion
  126.1 342.6 %psum.7 = f32[32]{0:T(128)S(1)} all-reduce(f32[32]{0:T(128)S(1)} %compare_select_fusion.1), channel_id=1, replica_groups=mesh['guide'=2,'seq'=128] {'seq'}, use_global_device_ids=true, to_apply=%region_31.32 | all-reduce | flops 32 | bytes 256 | tf_op jit(solution)/shard_map/psum | solution.py:138
  469.8 345.2 %pmax.7 = f32[1,32]{1,0:T(1,128)} all-reduce(f32[1,32]{1,0:T(1,128)S(1)} %fusion.97), channel_id=1, replica_groups=mesh['guide'=2,'seq'=128] {'seq'}, use_global_device_ids=true, to_apply=%region_33.34 | all-reduce | flops 32 | bytes 256 | tf_op jit(solution)/shard_map/pmax | solution.py:139
  815.0 1.3 multiply_add_fusion.6
  (81 shorter events, 15.0 us)
Async XLA Ops:
  7.2 116.5 %copy-start = (bf16[3072,64]{0,1:T(8,128)(2,1)S(1)}, bf16[3072,64]{0,1:T(8,128)(2,1)}, u32[]{:S(2)}) copy-start(bf16[3072,64]{0,1:T(8,128)(2,1)} %param.38) | copy-start | bytes 1179652
  7.2 1.1 copy-start.3
  7.2 109.9 %all-gather.2.cloned.1.call-start = ((), (), s32[]{:S(2)}) async-start(), calls=%async_computation | async-start | bytes 14155776 | tf_op jit(solution)/shard_map/all_gather | solution.py:128
  8.7 4.9 copy-start.8
  12.4 2.5 copy-start.1
  16.5 28.9 %collective-permute-start = (bf16[2,192,12,128]{3,1,2,0:T(8,128)(2,1)}, bf16[2,192,12,128]{3,1,2,0:T(8,128)(2,1)}, u32[]{:S(2)}, u32[]{:S(2)}) collective-permute-start(bf16[2,192,12,128]{3,1,2,0:T(8,128)(2,1)} %copy.61), channel_id=1, source_target_pairs={{0,32},{1,33},{2,34},{3,35},{4,36},{5,37},{6,38},{7,39},{8,40},{9,... | collective-permute-start | bytes 3538952 | tf_op jit(solution)/shard_map/ppermute | solution.py:19
  21.0 29.9 %collective-permute-start.3 = (bf16[2,192,12,128]{3,1,2,0:T(8,128)(2,1)}, bf16[2,192,12,128]{3,1,2,0:T(8,128)(2,1)}, u32[]{:S(2)}, u32[]{:S(2)}) collective-permute-start(bf16[2,192,12,128]{3,1,2,0:T(8,128)(2,1)} %copy.61), channel_id=1, source_target_pairs={{32,0},{33,1},{34,2},{35,3},{36,4},{37,5},{38,6},{39,7},{40,8},{41... | collective-permute-start | bytes 3538952 | tf_op jit(solution)/shard_map/ppermute | solution.py:19
  23.7 28.4 %copy-start.9 = (f32[128]{0:T(128)S(1)}, f32[128]{0:T(128)}, u32[]{:S(2)}) copy-start(f32[128]{0:T(128)} %param.32) | copy-start | bytes 1540
  26.5 27.7 %copy-start.10 = (s32[1,32]{1,0:T(1,128)S(1)}, s32[1,32]{1,0:T(1,128)}, u32[]{:S(2)}) copy-start(s32[1,32]{1,0:T(1,128)} %param.31) | copy-start | bytes 388
  26.5 29.0 %copy-start.2 = (bf16[192,12,128]{2,1,0:T(8,128)(2,1)S(1)}, bf16[192,12,128]{2,1,0:T(8,128)(2,1)}, u32[]{:S(2)}) copy-start(bf16[192,12,128]{2,1,0:T(8,128)(2,1)} %multiply_convert_fusion.1) | copy-start | bytes 1769476
  45.4 29.1 %collective-permute-start.1 = (bf16[2,192,12,128]{3,1,2,0:T(8,128)(2,1)}, bf16[2,192,12,128]{3,1,2,0:T(8,128)(2,1)}, u32[]{:S(2)}, u32[]{:S(2)}) collective-permute-start(bf16[2,192,12,128]{3,1,2,0:T(8,128)(2,1)} %collective-permute-done), channel_id=1, source_target_pairs={{0,32},{1,33},{2,34},{3,35},{4,36},{5,37},{6,38},{7,39},{8,40},{9,... | collective-permute-start | bytes 3538952 | tf_op jit(solution)/shard_map/ppermute | solution.py:19
  50.9 29.1 %collective-permute-start.4 = (bf16[2,192,12,128]{3,1,2,0:T(8,128)(2,1)}, bf16[2,192,12,128]{3,1,2,0:T(8,128)(2,1)}, u32[]{:S(2)}, u32[]{:S(2)}) collective-permute-start(bf16[2,192,12,128]{3,1,2,0:T(8,128)(2,1)} %collective-permute-done.3), channel_id=1, source_target_pairs={{32,0},{33,1},{34,2},{35,3},{36,4},{37,5},{38,6},{39,7},{40,8},{41... | collective-permute-start | bytes 3538952 | tf_op jit(solution)/shard_map/ppermute | solution.py:19
  56.6 25.7 %copy-start.11 = (f32[32]{0:T(128)S(1)}, f32[32]{0:T(128)}, u32[]{:S(2)}) copy-start(f32[32]{0:T(128)} %param.41) | copy-start | bytes 388
  74.5 28.2 %collective-permute-start.2 = (bf16[2,192,12,128]{3,1,2,0:T(8,128)(2,1)}, bf16[2,192,12,128]{3,1,2,0:T(8,128)(2,1)}, u32[]{:S(2)}, u32[]{:S(2)}) collective-permute-start(bf16[2,192,12,128]{3,1,2,0:T(8,128)(2,1)} %collective-permute-done.1), channel_id=1, source_target_pairs={{0,32},{1,33},{2,34},{3,35},{4,36},{5,37},{6,38},{7,39},{8,40},{9,... | collective-permute-start | bytes 3538952 | tf_op jit(solution)/shard_map/ppermute | solution.py:19
  79.9 32.4 %collective-permute-start.5 = (bf16[2,192,12,128]{3,1,2,0:T(8,128)(2,1)}, bf16[2,192,12,128]{3,1,2,0:T(8,128)(2,1)}, u32[]{:S(2)}, u32[]{:S(2)}) collective-permute-start(bf16[2,192,12,128]{3,1,2,0:T(8,128)(2,1)} %collective-permute-done.4), channel_id=1, source_target_pairs={{32,0},{33,1},{34,2},{35,3},{36,4},{37,5},{38,6},{39,7},{40,8},{41... | collective-permute-start | bytes 3538952 | tf_op jit(solution)/shard_map/ppermute | solution.py:19
  117.1 6.6 copy-start.6
  117.1 6.6 copy-start.7
  117.1 6.6 copy-start.12
  123.2 693.1 %copy-start.4 = (bf16[192,3072]{1,0:T(8,128)(2,1)}, bf16[192,3072]{1,0:T(8,128)(2,1)S(1)}, u32[]{:S(2)}) copy-start(bf16[192,3072]{1,0:T(8,128)(2,1)S(1)} %get-tuple-element.353) | copy-start | bytes 3538948
  123.2 691.8 %copy-start.5 = (f32[64,32]{0,1:T(8,128)S(1)}, f32[64,32]{0,1:T(8,128)}, u32[]{:S(2)}) copy-start(f32[64,32]{0,1:T(8,128)} %param.40) | copy-start | bytes 24580
  124.1 690.9 %collective-permute-start.6 = (f32[64,32]{0,1:T(8,128)S(1)}, f32[64,32]{0,1:T(8,128)S(1)}, u32[]{:S(2)}, u32[]{:S(2)}) collective-permute-start(f32[64,32]{0,1:T(8,128)S(1)} %constant_dynamic-slice_fusion), channel_id=1, source_target_pairs={{0,128},{128,0},{1,129},{129,1},{2,130},{130,2},{3,131},{131,3},{4... | collective-permute-start | bytes 24584 | tf_op jit(solution)/shard_map/ppermute | solution.py:29
Sparse Core Ops, SparseCore 0:
  9.8 29.8 all-gather.1
where the time goes:
time: 824 us; the launch traced here: 823 us
  blocking collectives  688 us (83%)
  waiting for transfers between devices  52.1 us (6%)
  matrix products  19.7 us (2%)
  starting transfers between devices  19.3 us (2%)
  other arithmetic  17.2 us (2%)
  between operations  14.6 us (2%)
  local copies, waits for them, and re-layouts  12.2 us (1%)
    pmax x1, blocking collectives, on_device(): peak_values = lax.pmax(peak_vector, 'seq')  345 us
    psum x1, blocking collectives, on_device(): square_sums = lax.psum(square_vector, 'seq')  343 us
    ppermute x6, waiting for transfers between devices, shifted(): lax.ppermute(value, axis, [(source, source + steps) for source in range(i...  51.4 us
    ppermute x6, starting transfers between devices, shifted(): lax.ppermute(value, axis, [(source, source + steps) for source in range(i...  19.1 us
  transfers between devices with their start and end apart: 8, of which 3 were waited for; matrix products, arithmetic and copies ran while one was open for 5% of the time, Pallas kernels for 0%

commit v1 on v0

v1 whole, which is shorter than its diff:
```python
import functools
import math

import jax
import jax.numpy as jnp
from jax import lax
from jax.experimental import pallas as pl
from jax.experimental.pallas import tpu as pltpu
from jax.sharding import PartitionSpec as P

HD = 128
GROUP = 4
TXT_DEV = 128
IMG_DEV = 64
BLOCK = TXT_DEV + IMG_DEV
HPD = 3
GUIDANCE = 3.5
ORDER = (2, 1, 3)


def normalize(rows, gain, factor):
    values = rows.astype(jnp.float32)
    inv = lax.rsqrt(jnp.mean(values * values, axis=-1, keepdims=True) + 1e-06)
    return (values * inv * gain * factor).astype(jnp.bfloat16)


def kernel(
    reqs,
    y_size,
    chunk,
    hidden,
    query,
    key,
    value,
    lengths,
    q_gain,
    k_gain,
    o_weight,
    gate,
    shift,
    scale,
    f_weight,
    f_bias,
    latents,
    delta,
    new_latents,
    hidden_out,
    rms_out,
    peak_out,
    qb,
    kb,
    vb,
    ob,
    att,
    wb,
    hid,
    outb,
    part,
    gate_b,
    shift_b,
    scale_b,
    fw_b,
    bias_b,
    lat_b,
    len_b,
    delta_b,
    qg_b,
    kg_b,
    vel_own,
    vel_got,
    st_x,
    st_y,
    st_z,
    in_send,
    in_recv,
    in_local,
    o_send,
    o_recv,
    w_send,
    w_recv,
    w_local,
    loc,
    out_sem,
    v_sem,
    s_send,
    s_recv,
):
    z_size = reqs // y_size
    width = hidden.shape[2]
    heads = GROUP * HPD
    g = lax.axis_index("guide")
    s = lax.axis_index("seq")
    x = s // reqs
    r = s % reqs
    y = r % y_size
    z = r // y_size

    def seq_of(xx, zz, yy):
        return xx * reqs + zz * y_size + yy

    def x_peer(o):
        return lax.rem(x + o, GROUP)

    def y_peer(o):
        return seq_of(x, z, lax.rem(y + o, y_size))

    def z_peer(o):
        return seq_of(x, lax.rem(z + o, z_size), y)

    tensors = ((key, kb), (value, vb), (query, qb))

    def columns(owner, h):
        return pl.ds(pl.multiple_of((owner * HPD + h) * HD, HD), HD)

    own = []
    for h in range(HPD):
        row = []
        for i, (src, dst) in enumerate(tensors):
            c = pltpu.make_async_copy(
                src.at[0, :, columns(x, h)], dst.at[h, x], in_local.at[i, h]
            )
            c.start()
            row.append(c)
        own.append(row)
    group8 = pl.ds(pl.multiple_of((r // 8) * 8, 8), 8) if reqs >= 8 else pl.ds(0, reqs)
    row8 = r % 8
    small = [
        (q_gain, qg_b),
        (k_gain, kg_b),
        (lengths, len_b),
        (gate.at[0, group8], gate_b),
        (hidden.at[0], hid),
        (shift.at[0, group8], shift_b),
        (scale.at[0, group8], scale_b),
        (f_weight, fw_b),
        (f_bias, bias_b),
        (latents, lat_b),
        (delta, delta_b),
    ]
    small = [pltpu.make_async_copy(a, b, loc.at[i]) for i, (a, b) in enumerate(small)]
    for c in small:
        c.start()

    barrier = pltpu.get_barrier_semaphore()
    for o in range(1, GROUP):
        pl.semaphore_signal(barrier, inc=1, device_id={"seq": seq_of(x_peer(o), z, y)})
    pl.semaphore_signal(barrier, inc=1, device_id={"guide": 1 - g})
    for o in range(1, y_size):
        pl.semaphore_signal(barrier, inc=1, device_id={"seq": y_peer(o)})
    for o in range(1, z_size):
        pl.semaphore_signal(barrier, inc=1, device_id={"seq": z_peer(o)})
    pl.semaphore_wait(barrier, GROUP + y_size - 1 + z_size - 1)

    def exchange(i, h, o):
        src, dst = tensors[i]
        t = x_peer(o)
        return pltpu.make_async_remote_copy(
            src_ref=src.at[0, :, columns(t, h)],
            dst_ref=dst.at[h, x],
            send_sem=in_send.at[i, h, o - 1],
            recv_sem=in_recv.at[i, h, o - 1],
            device_id={"seq": seq_of(t, z, y)},
        )

    for h in range(HPD):
        for i in range(3):
            for o in ORDER:
                exchange(i, h, o).start()

    def weight_pieces():
        first = (HPD - 1) * HD
        pieces = []
        for p in range(GROUP // 2):
            owner = g * (GROUP // 2) + p
            pieces.append((pl.ds(p * HPD * HD, first), pl.ds(pl.multiple_of(owner * first, HD), first)))
            pieces.append(
                (
                    pl.ds(p * HPD * HD + first, HD),
                    pl.ds(pl.multiple_of(GROUP * first + owner * HD, HD), HD),
                )
            )
        return pieces

    weight_sends, weight_locals = [], []
    for i, (a, b) in enumerate(weight_pieces()):
        c = pltpu.make_async_remote_copy(
            src_ref=o_weight.at[a],
            dst_ref=wb.at[b],
            send_sem=w_send.at[i],
            recv_sem=w_recv.at[i],
            device_id={"guide": 1 - g},
        )
        c.start()
        weight_sends.append(c)
        c = pltpu.make_async_copy(o_weight.at[a], wb.at[b], w_local.at[i])
        c.start()
        weight_locals.append(c)

    def give_back(h, o):
        t = x_peer(o)
        return pltpu.make_async_remote_copy(
            src_ref=ob.at[h, t],
            dst_ref=att.at[x * HPD + h],
            send_sem=o_send.at[h, o - 1],
            recv_sem=o_recv.at[h, o - 1],
            device_id={"seq": seq_of(t, z, y)},
        )

    for c in small[:3]:
        c.wait()
    lane = lax.broadcasted_iota(jnp.int32, (1, len_b.shape[1]), 1)
    length = jnp.sum(jnp.where(lane == r, len_b[...], 0), axis=1, keepdims=True)
    position = lax.broadcasted_iota(jnp.int32, (1, GROUP * BLOCK), 1)
    within = position % BLOCK
    usable = (within >= TXT_DEV) | ((position // BLOCK) * TXT_DEV + within < length)
    bias = jnp.where(usable, 0.0, -1e30).astype(jnp.float32)
    q_gain_row = qg_b[...]
    k_gain_row = kg_b[...]
    ones = jnp.ones((GROUP * BLOCK, HD), jnp.bfloat16)

    for h in range(HPD):
        for i in range(3):
            own[h][i].wait()
            for o in ORDER:
                exchange(i, h, o).wait_recv()
        keys = normalize(kb[h].reshape(GROUP * BLOCK, HD), k_gain_row, 1.0)
        values = jnp.concatenate([vb[h].reshape(GROUP * BLOCK, HD), ones], axis=1)
        for o in ORDER + (0,):
            t = x_peer(o)
            queries = normalize(qb[h, t], q_gain_row, 1.0 / math.sqrt(HD))
            scores = lax.dot_general(
                queries, keys, (((1,), (1,)), ((), ())), preferred_element_type=jnp.float32
            )
            scores = scores + bias
            top = jnp.max(scores, axis=1, keepdims=True)
            weights = jnp.exp(scores - top).astype(jnp.bfloat16)
            both = jnp.dot(weights, values, preferred_element_type=jnp.float32)
            result = (both[:, :HD] / both[:, HD:]).astype(jnp.bfloat16)
            if o == 0:
                att[x * HPD + h] = result
            else:
                ob[h, t] = result
                give_back(h, o).start()

    for c in weight_locals:
        c.wait()
    for c in weight_sends:
        c.wait_recv()
    for h in range(HPD - 1):
        for o in ORDER:
            give_back(h, o).wait_recv()
    depth = GROUP * (HPD - 1) * HD
    first = jnp.concatenate(
        [att[p * HPD + h] for p in range(GROUP) for h in range(HPD - 1)], axis=1
    )

    def first_part(n, carry):
        cols = pl.ds(pl.multiple_of(n * chunk, chunk), chunk)
        part[:, cols] = jnp.dot(first, wb[:depth, cols], preferred_element_type=jnp.float32)
        return carry

    lax.fori_loop(0, width // chunk, first_part, 0)

    for c in small[3:]:
        c.wait()
    for o in ORDER:
        give_back(HPD - 1, o).wait_recv()
    last = jnp.concatenate([att[p * HPD + HPD - 1] for p in range(GROUP)], axis=1)

    def out_copy(n):
        cols = pl.ds(pl.multiple_of(n * chunk, chunk), chunk)
        return pltpu.make_async_copy(outb.at[:, cols], hidden_out.at[0, :, cols], out_sem.at[n])

    def last_part(n, carry):
        squares, peaks, sums = carry
        cols = pl.ds(pl.multiple_of(n * chunk, chunk), chunk)
        projected = part[:, cols] + jnp.dot(
            last, wb[depth:, cols], preferred_element_type=jnp.float32
        )
        new = (hid[:, cols].astype(jnp.float32) + gate_b[pl.ds(row8, 1), cols] * projected).astype(
            jnp.bfloat16
        )
        outb[:, cols] = new
        out_copy(n).start()
        wide = new.astype(jnp.float32)
        folded = wide.reshape(BLOCK // 8, 8, chunk)
        squares = squares + jnp.sum(folded * folded, axis=0)
        peaks = jnp.maximum(peaks, jnp.max(jnp.abs(folded), axis=0))
        part_sums = wide[TXT_DEV:]
        part[TXT_DEV:, cols] = part_sums
        for k in range(chunk // 128):
            sums = sums + part_sums[:, k * 128 : (k + 1) * 128]
        return squares, peaks, sums

    zero = jnp.zeros((8, chunk), jnp.float32)
    squares, peaks, sums = lax.fori_loop(
        0, width // chunk, last_part, (zero, zero, jnp.zeros((IMG_DEV, 128), jnp.float32))
    )

    total = jnp.sum(jnp.sum(squares, axis=1, keepdims=True), axis=0, keepdims=True)
    peak = jnp.max(jnp.max(peaks, axis=1, keepdims=True), axis=0, keepdims=True)
    sub8 = lax.broadcasted_iota(jnp.int32, (8, 128), 0)
    lane8 = lax.broadcasted_iota(jnp.int32, (8, 128), 1)

    def stage(ref, slot, base, peers):
        copies = []
        for i, peer in enumerate(peers):
            c = pltpu.make_async_remote_copy(
                src_ref=ref.at[slot],
                dst_ref=ref.at[slot],
                send_sem=s_send.at[base + i],
                recv_sem=s_recv.at[base + i],
                device_id={"seq": peer},
            )
            c.start()
            copies.append(c)
        return copies

    st_x[x] = jnp.where(sub8 == 0, total, peak)
    x_copies = stage(st_x, x, 0, [seq_of(x_peer(o), z, y) for o in range(1, GROUP)])

    mean = jnp.sum(sums, axis=1, keepdims=True) * (1.0 / width)

    def variance(n, acc):
        cols = pl.ds(pl.multiple_of(n * chunk, chunk), chunk)
        centered = part[TXT_DEV:, cols] - mean
        centered = centered * centered
        for k in range(chunk // 128):
            acc = acc + centered[:, k * 128 : (k + 1) * 128]
        return acc

    var = lax.fori_loop(0, width // chunk, variance, jnp.zeros((IMG_DEV, 128), jnp.float32))
    inv = lax.rsqrt(jnp.sum(var, axis=1, keepdims=True) * (1.0 / width) + 1e-06)

    def velocity_part(n, acc):
        cols = pl.ds(pl.multiple_of(n * chunk, chunk), chunk)
        normed = (part[TXT_DEV:, cols] - mean) * inv
        mod = (
            normed * (1.0 + scale_b[pl.ds(row8, 1), cols]) + shift_b[pl.ds(row8, 1), cols]
        ).astype(jnp.bfloat16)
        return acc + jnp.dot(mod, fw_b[cols, :], preferred_element_type=jnp.float32)

    channels = fw_b.shape[1]
    velocity = lax.fori_loop(
        0, width // chunk, velocity_part, jnp.zeros((IMG_DEV, channels), jnp.float32)
    )
    velocity = velocity + bias_b[...]
    vel_own[...] = jnp.concatenate(
        [velocity, jnp.zeros((IMG_DEV, 128 - channels), jnp.float32)], axis=1
    )
    vel_copy = pltpu.make_async_remote_copy(
        src_ref=vel_own,
        dst_ref=vel_got,
        send_sem=v_sem.at[0],
        recv_sem=v_sem.at[1],
        device_id={"guide": 1 - g},
    )
    vel_copy.start()

    for c in x_copies:
        c.wait_recv()
    added, largest = st_x[0], st_x[0]
    for i in range(1, GROUP):
        added = added + st_x[i]
        largest = jnp.maximum(largest, st_x[i])
    st_y[y] = jnp.where(lane8 == r, jnp.where(sub8 == 0, added, largest), 0.0)
    y_copies = stage(st_y, y, GROUP - 1, [y_peer(o) for o in range(1, y_size)])

    vel_copy.wait_recv()
    mine, other = vel_own[...], vel_got[...]
    cond = jnp.where(g == 0, mine, other)
    uncond = jnp.where(g == 0, other, mine)
    guided = uncond + GUIDANCE * (cond - uncond)
    half = lat_b.shape[1]
    guided = jnp.where(g == 0, guided[:, :half], guided[:, half : 2 * half])
    step = jnp.sum(jnp.where(lane == r, delta_b[...], 0.0), axis=1, keepdims=True)
    new_latents[...] = lat_b[...] + step * guided

    for c in y_copies:
        c.wait_recv()
    added = st_y[0]
    for i in range(1, y_size):
        added = added + st_y[i]
    st_z[z] = added
    z_copies = stage(
        st_z, z, GROUP - 1 + y_size - 1, [z_peer(o) for o in range(1, z_size)]
    )
    for n in range(width // chunk):
        out_copy(n).wait()
    for h in range(HPD):
        for i in range(3):
            for o in ORDER:
                exchange(i, h, o).wait_send()
        for o in ORDER:
            give_back(h, o).wait_send()
    for c in weight_sends + x_copies + y_copies + [vel_copy]:
        c.wait_send()
    for c in z_copies:
        c.wait_recv()
    added = st_z[0]
    for i in range(1, z_size):
        added = added + st_z[i]
    count = GROUP * BLOCK * width
    rms_out[...] = jnp.sqrt(added[0:1, :reqs] / count + 1e-06)
    peak_out[...] = added[1:2, :reqs]
    for c in z_copies:
        c.wait_send()


def solution(mesh, y_size=4, chunk=512):
    reqs = mesh.shape["seq"] // GROUP

    def on_device(
        hidden,
        query_rows,
        key_rows,
        value_rows,
        text_lengths,
        q_gain,
        k_gain,
        o_weight,
        layer_gate,
        final_shift,
        final_scale,
        final_weight,
        final_bias,
        latents,
        step_delta,
    ):
        width = hidden.shape[2]
        heads = GROUP * HPD
        channels = final_weight.shape[1]
        z_size = reqs // y_size
        rows8 = min(8, reqs)
        bf16, f32 = jnp.bfloat16, jnp.float32
        vmem = pltpu.VMEM
        dma = pltpu.SemaphoreType.DMA
        stats = GROUP - 1 + y_size - 1 + z_size - 1
        any_spec = pl.BlockSpec(memory_space=pl.ANY)
        vmem_spec = pl.BlockSpec(memory_space=pltpu.VMEM)
        sds = jax.ShapeDtypeStruct
        return pl.pallas_call(
            functools.partial(kernel, reqs, y_size, chunk),
            out_shape=(
                sds(latents.shape, f32),
                sds(hidden.shape, bf16),
                sds((1, reqs), f32),
                sds((1, reqs), f32),
            ),
            in_specs=[any_spec] * 15,
            out_specs=(vmem_spec, any_spec, vmem_spec, vmem_spec),
            scratch_shapes=[
                vmem((HPD, GROUP, BLOCK, HD), bf16),
                vmem((HPD, GROUP, BLOCK, HD), bf16),
                vmem((HPD, GROUP, BLOCK, HD), bf16),
                vmem((HPD, GROUP, BLOCK, HD), bf16),
                vmem((heads, BLOCK, HD), bf16),
                vmem((heads * HD, width), bf16),
                vmem((BLOCK, width), bf16),
                vmem((BLOCK, width), bf16),
                vmem((BLOCK, width), f32),
                vmem((rows8, width), f32),
                vmem((rows8, width), f32),
                vmem((rows8, width), f32),
                vmem((width, channels), bf16),
                vmem((1, channels), f32),
                vmem(latents.shape, f32),
                vmem((1, reqs), jnp.int32),
                vmem((1, reqs), f32),
                vmem((1, HD), f32),
                vmem((1, HD), f32),
                vmem((IMG_DEV, 128), f32),
                vmem((IMG_DEV, 128), f32),
                vmem((GROUP, 8, 128), f32),
                vmem((y_size, 8, 128), f32),
                vmem((z_size, 8, 128), f32),
                dma((3, HPD, GROUP - 1)),
                dma((3, HPD, GROUP - 1)),
                dma((3, HPD)),
                dma((HPD, GROUP - 1)),
                dma((HPD, GROUP - 1)),
                dma((4,)),
                dma((4,)),
                dma((4,)),
                dma((11,)),
                dma((width // chunk,)),
                dma((2,)),
                dma((stats,)),
                dma((stats,)),
            ],
            compiler_params=pltpu.CompilerParams(
                collective_id=0, has_side_effects=True, vmem_limit_bytes=56 * 1024 * 1024
            ),
        )(
            hidden,
            query_rows,
            key_rows,
            value_rows,
            text_lengths,
            q_gain.reshape(1, -1),
            k_gain.reshape(1, -1),
            o_weight,
            layer_gate,
            final_shift,
            final_scale,
            final_weight,
            final_bias.reshape(1, -1),
            latents,
            step_delta.reshape(1, -1),
        )

    return jax.shard_map(
        on_device,
        mesh=mesh,
        in_specs=(
            P("guide", "seq", None),
            P("guide", "seq", None),
            P("guide", "seq", None),
            P("guide", "seq", None),
            P("guide", None),
            P(),
            P(),
            P("guide", None),
            P("guide", None, None),
            P("guide", None, None),
            P("guide", None, None),
            P(),
            P(),
            P("seq", "guide"),
            P(),
        ),
        out_specs=(P("seq", "guide"), P("guide", "seq", None), P("guide", None), P("guide", None)),
        check_vma=False,
    )
```

time: 824 us -> 61.5 us (0.07)
  blocking collectives: 688 us -> 0 us
  waiting for transfers between devices: 52.1 us -> 0 us
  Pallas kernels: 0 us -> 51.9 us
  matrix products: 19.7 us -> 0 us
  starting transfers between devices: 19.3 us -> 0 us
  other arithmetic: 17.2 us -> 0 us
  between operations: 14.6 us -> 0.64 us
    pmax x1 -> x0, blocking collectives: 345 us -> none  [on_device(): peak_values = lax.pmax(peak_vector, 'seq')]
    psum x1 -> x0, blocking collectives: 343 us -> none  [on_device(): square_sums = lax.psum(square_vector, 'seq')]
    pallas_call x0 -> x1, Pallas kernels: none -> 51.9 us  [on_device(): pl.pallas_call(functools.partial(kernel, reqs, y_size, chunk), out_shape=...]
    ppermute x7 -> x0, waiting for transfers between devices: 51.4 us -> none  [the longest x6 51.4 us: shifted(): lax.ppermute(value, axis, [(source, source + steps) for source in range(i...]
    dot_general x10 -> x0, matrix products: 19.7 us -> none  [the longest x4 7.91 us: attend(): jnp.einsum('hqk,khd->hqd', weights.astype(jnp.bfloat16), arrived[1], pref...]
    ppermute x7 -> x0, starting transfers between devices: 19.2 us -> none  [the longest x6 19.1 us: shifted(): lax.ppermute(value, axis, [(source, source + steps) for source in range(i...]
  transfers between devices with their start and end apart: 8 -> 0, of which waited for: 3 -> 0; matrix products, arithmetic and copies ran while one was open for 5% -> 0% of each run, Pallas kernels for 0% -> 0%
where the time goes in v1:
time: 61.5 us; the launch traced here: 61 us
  Pallas kernels  51.9 us (84%)
  local copies, waits for them, and re-layouts  8.4 us (14%)
  between operations  0.64 us (1%)
    pallas_call x1, Pallas kernels, on_device(): pl.pallas_call(functools.partial(kernel, reqs, y_size, chunk), out_shape=...  51.9 us
    unnamed x9, local copies, waits for them, and re-layouts  6.96 us
    pallas_call x1, local copies, waits for them, and re-layouts, on_device(): pl.pallas_call(functools.partial(kernel, reqs, y_size, chunk), out_shape=...  1.44 us

profile of v1, /device:TPU:8, one launch (start us, length us, event | category | flops | bytes accessed | tf_op | source)
XLA Modules:
  0.0 61.0 jit_solution(11372938681318029341)
XLA Ops:
  0.6 1.4 %copy.20.latents = f32[64,32]{1,0:T(8,128)} copy(f32[64,32]{0,1:T(8,128)} %param.28) | data formatting | bytes 16384 | tf_op args[13]
  2.0 2.2 %copy.19.f_weight = bf16[3072,64]{1,0:T(8,128)(2,1)} copy(bf16[3072,64]{0,1:T(8,128)(2,1)} %param.26) | data formatting | bytes 786432 | tf_op args[11]
  4.2 51.9 %shard_map.174 = (f32[64,32]{1,0:T(8,128)}, bf16[1,192,3072]{2,1,0:T(8,128)(2,1)}, f32[1,32]{1,0:T(1,128)}, f32[1,32]{1,0:T(1,128)}) custom-call(bf16[1,192,3072]{2,1,0:T(8,128)(2,1)} %hidden.1, bf16[1,192,1536]{2,1,0:T(8,128)(2,1)} %query.1, bf16[1,192,1536]{2,1,0:T(8,128)(2,1)} %key.1, bf16[1,192,1536]{2,1,0:T(8,128)(2,1)} %value.1, s32[1,32]{1,0:T(1,128)} %lengths.1, ...), custom_call_target="tpu_custom_call" | custom-call | tf_op jit(solution)/shard_map/pallas_call | solution.py:442
  56.1 1.4 %copy.21 = f32[64,32]{0,1:T(8,128)} copy(f32[64,32]{1,0:T(8,128)} %get-tuple-element.4) | data formatting | bytes 16384 | tf_op jit(solution)/shard_map/pallas_call | solution.py:442
  57.6 0.0 copy-start.1
  57.6 0.0 copy-start
  57.6 2.4 %copy.25 = bf16[1,192,3072]{2,1,0:T(8,128)(2,1)} copy(bf16[1,192,3072]{2,1,0:T(8,128)(2,1)} %get-tuple-element.13) | data formatting | bytes 2359296
  59.9 0.0 copy-done.1
  59.9 0.5 copy.26
  60.5 0.0 copy-done
  60.5 0.5 copy.27
Async XLA Ops:
  57.6 2.4 %copy-start.1 = (f32[1,32]{1,0:T(1,128)S(1)}, f32[1,32]{1,0:T(1,128)}, u32[]{:S(2)}) copy-start(f32[1,32]{1,0:T(1,128)} %get-tuple-element.14) | copy-start | bytes 388
  57.6 2.9 %copy-start = (f32[1,32]{1,0:T(1,128)S(1)}, f32[1,32]{1,0:T(1,128)}, u32[]{:S(2)}) copy-start(f32[1,32]{1,0:T(1,128)} %get-tuple-element.15) | copy-start | bytes 388

commit v2 on v1

--- a/solution.py
+++ b/solution.py
@@ -54,7 +54,6 @@
     att,
     wb,
     hid,
-    outb,
     part,
     gate_b,
     shift_b,
@@ -68,8 +67,7 @@
     kg_b,
     vel_own,
     vel_got,
-    st_x,
-    st_y,
+    st_p,
     st_z,
     in_send,
     in_recv,
@@ -80,7 +78,6 @@
     w_recv,
     w_local,
     loc,
-    out_sem,
     v_sem,
     s_send,
     s_recv,
@@ -101,11 +98,16 @@
     def x_peer(o):
         return lax.rem(x + o, GROUP)
 
-    def y_peer(o):
-        return seq_of(x, z, lax.rem(y + o, y_size))
-
     def z_peer(o):
         return seq_of(x, lax.rem(z + o, z_size), y)
+
+    plane = [(i, j) for i in range(GROUP) for j in range(y_size) if i + j > 0]
+    plane = [seq_of(x_peer(i), z, lax.rem(y + j, y_size)) for i, j in plane]
+    z_peers = [z_peer(o) for o in range(1, z_size)]
+    barrier = pltpu.get_barrier_semaphore()
+    pl.semaphore_signal(barrier, inc=1, device_id={"guide": 1 - g})
+    for peer in plane + z_peers:
+        pl.semaphore_signal(barrier, inc=1, device_id={"seq": peer})
 
     tensors = ((key, kb), (value, vb), (query, qb))
 
@@ -141,15 +143,7 @@
     for c in small:
         c.start()
 
-    barrier = pltpu.get_barrier_semaphore()
-    for o in range(1, GROUP):
-        pl.semaphore_signal(barrier, inc=1, device_id={"seq": seq_of(x_peer(o), z, y)})
-    pl.semaphore_signal(barrier, inc=1, device_id={"guide": 1 - g})
-    for o in range(1, y_size):
-        pl.semaphore_signal(barrier, inc=1, device_id={"seq": y_peer(o)})
-    for o in range(1, z_size):
-        pl.semaphore_signal(barrier, inc=1, device_id={"seq": z_peer(o)})
-    pl.semaphore_wait(barrier, GROUP + y_size - 1 + z_size - 1)
+    pl.semaphore_wait(barrier, len(plane) + len(z_peers) + 1)
 
     def exchange(i, h, o):
         src, dst = tensors[i]
@@ -267,10 +261,6 @@
         give_back(HPD - 1, o).wait_recv()
     last = jnp.concatenate([att[p * HPD + HPD - 1] for p in range(GROUP)], axis=1)
 
-    def out_copy(n):
-        cols = pl.ds(pl.multiple_of(n * chunk, chunk), chunk)
-        return pltpu.make_async_copy(outb.at[:, cols], hidden_out.at[0, :, cols], out_sem.at[n])
-
     def last_part(n, carry):
         squares, peaks, sums = carry
         cols = pl.ds(pl.multiple_of(n * chunk, chunk), chunk)
@@ -280,8 +270,7 @@
         new = (hid[:, cols].astype(jnp.float32) + gate_b[pl.ds(row8, 1), cols] * projected).astype(
             jnp.bfloat16
         )
-        outb[:, cols] = new
-        out_copy(n).start()
+        hidden_out[0, :, cols] = new
         wide = new.astype(jnp.float32)
         folded = wide.reshape(BLOCK // 8, 8, chunk)
         squares = squares + jnp.sum(folded * folded, axis=0)
@@ -316,8 +305,9 @@
             copies.append(c)
         return copies
 
-    st_x[x] = jnp.where(sub8 == 0, total, peak)
-    x_copies = stage(st_x, x, 0, [seq_of(x_peer(o), z, y) for o in range(1, GROUP)])
+    here = x * y_size + y
+    st_p[here] = jnp.where(lane8 == r, jnp.where(sub8 == 0, total, peak), 0.0)
+    p_copies = stage(st_p, here, 0, plane)
 
     mean = jnp.sum(sums, axis=1, keepdims=True) * (1.0 / width)
 
@@ -338,9 +328,11 @@
         mod = (
             normed * (1.0 + scale_b[pl.ds(row8, 1), cols]) + shift_b[pl.ds(row8, 1), cols]
         ).astype(jnp.bfloat16)
-        return acc + jnp.dot(mod, fw_b[cols, :], preferred_element_type=jnp.float32)
-
-    channels = fw_b.shape[1]
+        return acc + lax.dot_general(
+            mod, fw_b[:, cols], (((1,), (1,)), ((), ())), preferred_element_type=jnp.float32
+        )
+
+    channels = fw_b.shape[0]
     velocity = lax.fori_loop(
         0, width // chunk, velocity_part, jnp.zeros((IMG_DEV, channels), jnp.float32)
     )
@@ -357,43 +349,33 @@
     )
     vel_copy.start()
 
-    for c in x_copies:
+    for c in p_copies:
         c.wait_recv()
-    added, largest = st_x[0], st_x[0]
-    for i in range(1, GROUP):
-        added = added + st_x[i]
-        largest = jnp.maximum(largest, st_x[i])
-    st_y[y] = jnp.where(lane8 == r, jnp.where(sub8 == 0, added, largest), 0.0)
-    y_copies = stage(st_y, y, GROUP - 1, [y_peer(o) for o in range(1, y_size)])
+    added, largest = st_p[0], st_p[0]
+    for i in range(1, GROUP * y_size):
+        added = added + st_p[i]
+        largest = jnp.maximum(largest, st_p[i])
+    st_z[z] = jnp.where(sub8 == 0, added, largest)
+    z_copies = stage(st_z, z, len(plane), z_peers)
 
     vel_copy.wait_recv()
     mine, other = vel_own[...], vel_got[...]
     cond = jnp.where(g == 0, mine, other)
     uncond = jnp.where(g == 0, other, mine)
     guided = uncond + GUIDANCE * (cond - uncond)
-    half = lat_b.shape[1]
-    guided = jnp.where(g == 0, guided[:, :half], guided[:, half : 2 * half])
+    half = lat_b.shape[0]
+    guided = guided.T
+    guided = jnp.where(g == 0, guided[:half], guided[half : 2 * half])
     step = jnp.sum(jnp.where(lane == r, delta_b[...], 0.0), axis=1, keepdims=True)
     new_latents[...] = lat_b[...] + step * guided
 
-    for c in y_copies:
-        c.wait_recv()
-    added = st_y[0]
-    for i in range(1, y_size):
-        added = added + st_y[i]
-    st_z[z] = added
-    z_copies = stage(
-        st_z, z, GROUP - 1 + y_size - 1, [z_peer(o) for o in range(1, z_size)]
-    )
-    for n in range(width // chunk):
-        out_copy(n).wait()
     for h in range(HPD):
         for i in range(3):
             for o in ORDER:
                 exchange(i, h, o).wait_send()
         for o in ORDER:
             give_back(h, o).wait_send()
-    for c in weight_sends + x_copies + y_copies + [vel_copy]:
+    for c in weight_sends + p_copies + [vel_copy]:
         c.wait_send()
     for c in z_copies:
         c.wait_recv()
@@ -407,7 +389,16 @@
         c.wait_send()
 
 
-def solution(mesh, y_size=4, chunk=512):
+def write_out(latents, hidden, rms, peak, latents_out, hidden_out, rms_out, peak_out, sems):
+    pairs = ((hidden, hidden_out), (latents, latents_out), (rms, rms_out), (peak, peak_out))
+    copies = [pltpu.make_async_copy(a, b, sems.at[i]) for i, (a, b) in enumerate(pairs)]
+    for c in copies:
+        c.start()
+    for c in copies:
+        c.wait()
+
+
+def solution(mesh, y_size=4, chunk=3072):
     reqs = mesh.shape["seq"] // GROUP
 
     def on_device(
@@ -435,20 +426,21 @@
         bf16, f32 = jnp.bfloat16, jnp.float32
         vmem = pltpu.VMEM
         dma = pltpu.SemaphoreType.DMA
-        stats = GROUP - 1 + y_size - 1 + z_size - 1
-        any_spec = pl.BlockSpec(memory_space=pl.ANY)
+        stats = GROUP * y_size - 1 + z_size - 1
+        any_spec = pl.BlockSpec(memory_space=pltpu.HBM)
         vmem_spec = pl.BlockSpec(memory_space=pltpu.VMEM)
         sds = jax.ShapeDtypeStruct
-        return pl.pallas_call(
+        results = (
+            sds(latents.shape[::-1], f32),
+            sds(hidden.shape, bf16),
+            sds((1, reqs), f32),
+            sds((1, reqs), f32),
+        )
+        new, out, rms, peak = pl.pallas_call(
             functools.partial(kernel, reqs, y_size, chunk),
-            out_shape=(
-                sds(latents.shape, f32),
-                sds(hidden.shape, bf16),
-                sds((1, reqs), f32),
-                sds((1, reqs), f32),
-            ),
+            out_shape=tuple(vmem(v.shape, v.dtype) for v in results),
             in_specs=[any_spec] * 15,
-            out_specs=(vmem_spec, any_spec, vmem_spec, vmem_spec),
+            out_specs=(vmem_spec,) * 4,
             scratch_shapes=[
                 vmem((HPD, GROUP, BLOCK, HD), bf16),
                 vmem((HPD, GROUP, BLOCK, HD), bf16),
@@ -457,22 +449,20 @@
                 vmem((heads, BLOCK, HD), bf16),
                 vmem((heads * HD, width), bf16),
                 vmem((BLOCK, width), bf16),
-                vmem((BLOCK, width), bf16),
                 vmem((BLOCK, width), f32),
                 vmem((rows8, width), f32),
                 vmem((rows8, width), f32),
                 vmem((rows8, width), f32),
-                vmem((width, channels), bf16),
+                vmem((channels, width), bf16),
                 vmem((1, channels), f32),
-                vmem(latents.shape, f32),
+                vmem(latents.shape[::-1], f32),
                 vmem((1, reqs), jnp.int32),
                 vmem((1, reqs), f32),
                 vmem((1, HD), f32),
                 vmem((1, HD), f32),
                 vmem((IMG_DEV, 128), f32),
                 vmem((IMG_DEV, 128), f32),
-                vmem((GROUP, 8, 128), f32),
-                vmem((y_size, 8, 128), f32),
+                vmem((GROUP * y_size, 8, 128), f32),
                 vmem((z_size, 8, 128), f32),
                 dma((3, HPD, GROUP - 1)),
                 dma((3, HPD, GROUP - 1)),
@@ -483,31 +473,43 @@
                 dma((4,)),
                 dma((4,)),
                 dma((11,)),
-                dma((width // chunk,)),
                 dma((2,)),
                 dma((stats,)),
                 dma((stats,)),
             ],
             compiler_params=pltpu.CompilerParams(
-                collective_id=0, has_side_effects=True, vmem_limit_bytes=56 * 1024 * 1024
+                collective_id=0, has_side_effects=True, vmem_limit_bytes=48 * 1024 * 1024
             ),
         )(
-            hidden,
-            query_rows,
-            key_rows,
-            value_rows,
-            text_lengths,
-            q_gain.reshape(1, -1),
-            k_gain.reshape(1, -1),
-            o_weight,
-            layer_gate,
-            final_shift,
-            final_scale,
-            final_weight,
-            final_bias.reshape(1, -1),
-            latents,
-            step_delta.reshape(1, -1),
-        )
+            *(
+                pltpu.with_memory_space_constraint(v, pltpu.HBM)
+                for v in (
+                    hidden,
+                    query_rows,
+                    key_rows,
+                    value_rows,
+                    text_lengths,
+                    q_gain.reshape(1, -1),
+                    k_gain.reshape(1, -1),
+                    o_weight,
+                    layer_gate,
+                    final_shift,
+                    final_scale,
+                    final_weight.T,
+                    final_bias.reshape(1, -1),
+                    latents.T,
+                    step_delta.reshape(1, -1),
+                )
+            )
+        )
+        new, out, rms, peak = pl.pallas_call(
+            write_out,
+            out_shape=tuple(pltpu.HBM(v.shape, v.dtype) for v in results),
+            in_specs=[vmem_spec] * 4,
+            out_specs=[any_spec] * 4,
+            scratch_shapes=[dma((4,))],
+        )(*(pltpu.with_memory_space_constraint(v, pltpu.VMEM) for v in (new, out, rms, peak)))
+        return new.T, out, rms, peak
 
     return jax.shard_map(
         on_device,

time: 61.5 us -> 50.4 us (0.82)
  local copies, waits for them, and re-layouts: 8.4 us -> 0 us
  Pallas kernels: 51.9 us -> 49.7 us
    unnamed x9 -> x0, local copies, waits for them, and re-layouts: 6.96 us -> none
    pallas_call x1, Pallas kernels: 51.9 us -> 48.7 us  [on_device(): pl.pallas_call(functools.partial(kernel, reqs, y_size, chunk), out_shape=...]
    pallas_call x1 -> x0, local copies, waits for them, and re-layouts: 1.44 us -> none  [on_device(): pl.pallas_call(functools.partial(kernel, reqs, y_size, chunk), out_shape=...]
    pallas_call x0 -> x1, Pallas kernels: none -> 1.06 us  [on_device(): pl.pallas_call(write_out, out_shape=tuple((pltpu.HBM(v.shape, v.dtype) fo...]
where the time goes in v2:
time: 50.4 us
  Pallas kernels  49.7 us (99%)
  between operations  0.65 us (1%)
    pallas_call x1, Pallas kernels, on_device(): pl.pallas_call(functools.partial(kernel, reqs, y_size, chunk), out_shape=...  48.7 us
    pallas_call x1, Pallas kernels, on_device(): pl.pallas_call(write_out, out_shape=tuple((pltpu.HBM(v.shape, v.dtype) fo...  1.06 us

profile of v2, /device:TPU:8, one launch (start us, length us, event | category | flops | bytes accessed | tf_op | source)
XLA Modules:
  0.0 50.4 jit_solution(7429265323536441891)
XLA Ops:
  0.6 48.7 %shard_map.174 = (f32[32,64]{1,0:T(8,128)S(1)}, bf16[1,192,3072]{2,1,0:T(8,128)(2,1)S(1)}, f32[1,32]{1,0:T(1,128)S(1)}, f32[1,32]{1,0:T(1,128)S(1)}) custom-call(bf16[1,192,3072]{2,1,0:T(8,128)(2,1)} %hidden.1, bf16[1,192,1536]{2,1,0:T(8,128)(2,1)} %query.1, bf16[1,192,1536]{2,1,0:T(8,128)(2,1)} %key.1, bf16[1,192,1536]{2,1,0:T(8,128)(2,1)} %value.1, ...), custom_call_target="tpu_custom_call" | custom-call | tf_op jit(solution)/shard_map/pallas_call | solution.py:439
  49.3 1.1 %shard_map.175 = (f32[32,64]{1,0:T(8,128)}, bf16[1,192,3072]{2,1,0:T(8,128)(2,1)}, f32[1,32]{1,0:T(1,128)}, f32[1,32]{1,0:T(1,128)}) custom-call(f32[32,64]{1,0:T(8,128)S(1)} %get-tuple-element.12.latents, bf16[1,192,3072]{2,1,0:T(8,128)(2,1)S(1)} %get-tuple-element.13.hidden, f32[1,32]{1,0:T(1,128)S(1)} %get-tuple-element.14.rms, ...), custom_call_target="tpu_custom_call" | custom-call | tf_op jit(solution)/shard_map/pallas_call | solution.py:505

commit v3 on v2

--- a/solution.py
+++ b/solution.py
@@ -102,8 +102,9 @@
         return seq_of(x, lax.rem(z + o, z_size), y)
 
     plane = [(i, j) for i in range(GROUP) for j in range(y_size) if i + j > 0]
+    plane.sort(key=lambda p: -min(p[0], GROUP - p[0]) - min(p[1], y_size - p[1]))
     plane = [seq_of(x_peer(i), z, lax.rem(y + j, y_size)) for i, j in plane]
-    z_peers = [z_peer(o) for o in range(1, z_size)]
+    z_peers = [z_peer(o) for o in sorted(range(1, z_size), key=lambda o: -min(o, z_size - o))]
     barrier = pltpu.get_barrier_semaphore()
     pl.semaphore_signal(barrier, inc=1, device_id={"guide": 1 - g})
     for peer in plane + z_peers:
@@ -156,10 +157,18 @@
             device_id={"seq": seq_of(t, z, y)},
         )
 
-    for h in range(HPD):
-        for i in range(3):
-            for o in ORDER:
-                exchange(i, h, o).start()
+    pieces = [(i, h, o) for h in range(HPD) for i in range(3) for o in ORDER]
+    now = 11
+
+    def send(some):
+        for i, h, o in some:
+            exchange(i, h, o).start()
+
+    send(pieces[:now])
+
+    @pl.when(g == 0)
+    def _():
+        send(pieces[now:])
 
     def weight_pieces():
         first = (HPD - 1) * HD
@@ -217,6 +226,12 @@
             own[h][i].wait()
             for o in ORDER:
                 exchange(i, h, o).wait_recv()
+        if h == 0:
+
+            @pl.when(g == 1)
+            def _():
+                send(pieces[now:])
+
         keys = normalize(kb[h].reshape(GROUP * BLOCK, HD), k_gain_row, 1.0)
         values = jnp.concatenate([vb[h].reshape(GROUP * BLOCK, HD), ones], axis=1)
         for o in ORDER + (0,):
@@ -288,8 +303,7 @@
 
     total = jnp.sum(jnp.sum(squares, axis=1, keepdims=True), axis=0, keepdims=True)
     peak = jnp.max(jnp.max(peaks, axis=1, keepdims=True), axis=0, keepdims=True)
-    sub8 = lax.broadcasted_iota(jnp.int32, (8, 128), 0)
-    lane8 = lax.broadcasted_iota(jnp.int32, (8, 128), 1)
+    lanes = lax.broadcasted_iota(jnp.int32, (1, 128), 1)
 
     def stage(ref, slot, base, peers):
         copies = []
@@ -306,7 +320,7 @@
         return copies
 
     here = x * y_size + y
-    st_p[here] = jnp.where(lane8 == r, jnp.where(sub8 == 0, total, peak), 0.0)
+    st_p[here] = jnp.where(lanes == r, total, jnp.where(lanes == 64 + r, peak, 0.0))
     p_copies = stage(st_p, here, 0, plane)
 
     mean = jnp.sum(sums, axis=1, keepdims=True) * (1.0 / width)
@@ -355,7 +369,7 @@
     for i in range(1, GROUP * y_size):
         added = added + st_p[i]
         largest = jnp.maximum(largest, st_p[i])
-    st_z[z] = jnp.where(sub8 == 0, added, largest)
+    st_z[z] = jnp.where(lanes < 64, added, largest)
     z_copies = stage(st_z, z, len(plane), z_peers)
 
     vel_copy.wait_recv()
@@ -383,8 +397,8 @@
     for i in range(1, z_size):
         added = added + st_z[i]
     count = GROUP * BLOCK * width
-    rms_out[...] = jnp.sqrt(added[0:1, :reqs] / count + 1e-06)
-    peak_out[...] = added[1:2, :reqs]
+    rms_out[...] = jnp.sqrt(added[:, :reqs] / count + 1e-06)
+    peak_out[...] = added[:, 64 : 64 + reqs]
     for c in z_copies:
         c.wait_send()
 
@@ -462,8 +476,8 @@
                 vmem((1, HD), f32),
                 vmem((IMG_DEV, 128), f32),
                 vmem((IMG_DEV, 128), f32),
-                vmem((GROUP * y_size, 8, 128), f32),
-                vmem((z_size, 8, 128), f32),
+                vmem((GROUP * y_size, 1, 128), f32),
+                vmem((z_size, 1, 128), f32),
                 dma((3, HPD, GROUP - 1)),
                 dma((3, HPD, GROUP - 1)),
                 dma((3, HPD)),

time: 50.4 us -> 49.8 us (0.988)
  Pallas kernels: 49.7 us -> 48.9 us
    pallas_call x1, Pallas kernels: 48.7 us -> 47.9 us  [on_device(): pl.pallas_call(functools.partial(kernel, reqs, y_size, chunk), out_shape=...]
where the time goes in v3:
time: 49.8 us; the launch traced here: 49.6 us
  Pallas kernels  48.9 us (98%)
  between operations  0.65 us (1%)
    pallas_call x1, Pallas kernels, on_device(): pl.pallas_call(functools.partial(kernel, reqs, y_size, chunk), out_shape=...  47.9 us
    pallas_call x1, Pallas kernels, on_device(): pl.pallas_call(write_out, out_shape=tuple((pltpu.HBM(v.shape, v.dtype) fo...  1.06 us

profile of v3, /device:TPU:8, one launch (start us, length us, event | category | flops | bytes accessed | tf_op | source)
XLA Modules:
  0.0 49.6 jit_solution(15739540810173891181)
XLA Ops:
  0.6 47.9 %shard_map.174 = (f32[32,64]{1,0:T(8,128)S(1)}, bf16[1,192,3072]{2,1,0:T(8,128)(2,1)S(1)}, f32[1,32]{1,0:T(1,128)S(1)}, f32[1,32]{1,0:T(1,128)S(1)}) custom-call(bf16[1,192,3072]{2,1,0:T(8,128)(2,1)} %hidden.1, bf16[1,192,1536]{2,1,0:T(8,128)(2,1)} %query.1, bf16[1,192,1536]{2,1,0:T(8,128)(2,1)} %key.1, bf16[1,192,1536]{2,1,0:T(8,128)(2,1)} %value.1, ...), custom_call_target="tpu_custom_call" | custom-call | tf_op jit(solution)/shard_map/pallas_call | solution.py:453
  48.5 1.1 %shard_map.175 = (f32[32,64]{1,0:T(8,128)}, bf16[1,192,3072]{2,1,0:T(8,128)(2,1)}, f32[1,32]{1,0:T(1,128)}, f32[1,32]{1,0:T(1,128)}) custom-call(f32[32,64]{1,0:T(8,128)S(1)} %get-tuple-element.12.latents, bf16[1,192,3072]{2,1,0:T(8,128)(2,1)S(1)} %get-tuple-element.13.hidden, f32[1,32]{1,0:T(1,128)S(1)} %get-tuple-element.14.rms, ...), custom_call_target="tpu_custom_call" | custom-call | tf_op jit(solution)/shard_map/pallas_call | solution.py:519
